TPU v7x, 32 devices: a whole 2x2x4 slice. The times are simulated.
32 devices in a mesh: seq: 16 (over z, x, core), head: 2 (over y).
Axes of the slice: x: 2, y: 2, z: 4, core: 2. Of those that a mesh axis runs over, the one named last changes fastest.
Arguments:
- qkv: bfloat16 [3, 8192, 4096], P(None, ('seq', 'head')), may hold values from -6 to 6
- send_rows: int32 [16, 16, 40], P('seq'), may hold values from -1 to 511, as said below
- recv_pos: int32 [16, 16, 40], P('seq'), may hold values from -1 to 511, as said below
- req_lengths: int32 [4], replicated, may hold values from 1 to 4096, 8192 in all
- norm_gain: float32 [4096], P('head'), may hold values from 0.5 to 1.5
Outputs:
- attn_out: bfloat16 [8192, 4096], P('seq', 'head')
Inputs may be any that keep to these rules, and one draw needn't show every extreme that they name: send_rows[l, o, c] is a row of loader group l (rows l * 512 to l * 512 + 511 of qkv, counted from the group's first) sent to owner o in slot c, or -1 for an empty slot; used slots come first. Every row of a group is sent exactly once. At most 40 rows go from one group to one owner, and in every draw some pairs carry exactly 40, so that every group sends and every owner receives 40 rows from one pair. The number of rows from group l to owner o depends only on (o - l) modulo the number of groups. recv_pos[o, l, c] is the position within owner o's block of 512 packed positions where slot c from group l lands, and -1 exactly where send_rows[l, o, c] is -1; every position of a block is filled exactly once.
All inputs are finite; a program needn't handle non-finite values.
Results may differ from a plain program's by a relative error of at most 0.003.
Values may be sent and summed in bfloat16 or wider, within the bound.
No kernel may reach another device: no remote copies, remote signals or barrier semaphores. Data moves between devices by JAX's collectives and lax.ppermute only.
A program may use at most 128 MiB of HBM per device.

v0:
```python
import jax
import jax.numpy as jnp
from jax import lax
from jax.sharding import PartitionSpec as P

HEAD_DIM = 128
norm_eps = 1e-06


def prefix(shard, axis, combine, identity):
    length, position = (lax.axis_size(axis), lax.axis_index(axis))
    everything = jax.tree.map(lambda part: lax.all_gather(part, axis), shard)
    start = jax.tree.map(
        lambda part, zero: jnp.broadcast_to(jnp.asarray(zero, part.dtype), part.shape),
        shard,
        identity,
    )

    def lap(k, before):
        reached = k < position
        new = combine(before, jax.tree.map(lambda part: part[k], everything))
        return jax.tree.map(lambda a, b: jnp.where(reached, a, b), new, before)

    return lax.fori_loop(0, length, lap, start)


def place_rows(incoming, land_rows, tok_rows):
    row_width = incoming.shape[-1]
    planes = incoming.shape[0]
    flat_rows = incoming.reshape(planes, -1, row_width)
    land_index = jnp.where(land_rows < 0, tok_rows, land_rows).reshape(-1)
    blank_rows = jnp.zeros((planes, tok_rows, row_width), incoming.dtype)
    return blank_rows.at[:, land_index].set(flat_rows, mode="drop")


def carry_combine(earlier, later):
    return (later[0] + (1.0 - later[1]) * earlier[0], jnp.maximum(earlier[1], later[1]))


def on_device(qkv, send_rows, recv_pos, req_lengths, norm_gain):
    seq_count = lax.axis_size("seq")
    slot_count = send_rows.shape[2]
    pick_rows = jnp.maximum(send_rows[0], 0).reshape(-1)
    land_rows = recv_pos[0]
    grouped = lax.all_to_all(qkv, "head", split_axis=2, concat_axis=1, tiled=True)
    outgoing = jnp.take(grouped, pick_rows, axis=1).reshape(
        3, seq_count, slot_count, grouped.shape[2]
    )
    arrived = lax.all_to_all(outgoing, "seq", split_axis=1, concat_axis=1, tiled=True)
    packed = place_rows(arrived, land_rows, grouped.shape[1])
    query, keys, values = (packed[0], packed[1], packed[2])
    tok_rows = keys.shape[0]
    head_count = keys.shape[1] // HEAD_DIM
    first_row = lax.axis_index("seq") * tok_rows
    req_ends = jnp.cumsum(req_lengths)
    req_starts = req_ends - req_lengths
    positions = first_row + jnp.arange(tok_rows, dtype=jnp.int32)
    segment = jnp.sum((req_starts[None, :] <= positions[:, None]).astype(jnp.int32), axis=1) - 1
    prev_segment = jnp.sum((req_starts < first_row).astype(jnp.int32)) - 1
    inside = jnp.any((req_starts >= first_row) & (req_starts < first_row + tok_rows))
    has_start = jnp.where(inside, 1.0, 0.0).astype(jnp.float32)
    carried_mask = segment == prev_segment
    tail_mask = segment == segment[tok_rows - 1]
    causal = (positions[None, :] <= positions[:, None]) & (segment[None, :] == segment[:, None])
    tail_keys = jnp.where(tail_mask[:, None], keys, jnp.zeros_like(keys))
    update = jnp.einsum(
        "shd,she->hde",
        tail_keys.reshape(tok_rows, head_count, HEAD_DIM),
        values.reshape(tok_rows, head_count, HEAD_DIM),
        preferred_element_type=jnp.float32,
    )
    identity = (jnp.zeros_like(update), jnp.zeros((), jnp.float32))
    carried_pair = prefix((update, has_start), "seq", carry_combine, identity)
    carried = carried_pair[0]
    outputs = []
    for number in range(head_count):
        columns = slice(number * HEAD_DIM, (number + 1) * HEAD_DIM)
        query_head = query[:, columns]
        key_head = keys[:, columns]
        value_head = values[:, columns]
        scores = lax.dot_general(
            query_head, key_head, (((1,), (1,)), ((), ())), preferred_element_type=jnp.float32
        )
        weights = jnp.where(causal, scores, 0.0).astype(jnp.bfloat16)
        local_term = jnp.dot(weights, value_head, preferred_element_type=jnp.float32)
        carried_term = jnp.dot(
            query_head.astype(jnp.float32),
            carried[number],
            precision=lax.Precision.HIGHEST,
            preferred_element_type=jnp.float32,
        )
        raw_out = local_term + jnp.where(carried_mask[:, None], carried_term, 0.0)
        inv_rms = lax.rsqrt(jnp.mean(raw_out * raw_out, axis=1, keepdims=True) + norm_eps)
        outputs.append((raw_out * inv_rms * norm_gain[columns][None, :]).astype(jnp.bfloat16))
    return jnp.concatenate(outputs, axis=1)


def solution(mesh):
    return jax.shard_map(
        on_device,
        mesh=mesh,
        in_specs=(
            P(None, ("seq", "head"), None),
            P("seq", None, None),
            P("seq", None, None),
            P(),
            P("head"),
        ),
        out_specs=P("seq", "head"),
        check_vma=False,
    )
```

profile of v0, /device:TPU:0, one launch (start us, length us, event | category | flops | bytes accessed | tf_op | source)
XLA Modules:
  0.0 782.3 jit_solution(8094631923778563405)
XLA Ops:
  6.5 13.1 %copy.40 = bf16[3,256,4096]{1,0,2:T(4,128)(2,1)} copy(bf16[3,256,4096]{2,1,0:T(8,128)(2,1)} %param.7) | data formatting | bytes 12582912 | tf_op args[0]
  19.6 7.1 all-to-all-start
  26.8 93.7 %all-to-all-done = bf16[3,256,4096]{1,0,2:T(4,128)(2,1)} async-done(((bf16[3,256,4096]{1,0,2:T(4,128)(2,1)}), bf16[3,256,4096]{1,0,2:T(4,128)(2,1)}, u32[]{:S(2)}, u32[]{:S(2)}) %all-to-all-start) | async-done | bytes 6291488 | tf_op jit(solution)/shard_map/all_to_all | solution.py:45
  120.6 7.0 copy.41
  127.5 8.7 %copy.42 = bf16[3,2,256,2048]{3,2,1,0:T(8,128)(2,1)} copy(bf16[3,2,256,2048]{2,3,1,0:T(8,128)(2,1)} %bitcast.90) | data formatting | bytes 12582912 | tf_op jit(solution)/shard_map/all_to_all | solution.py:45
  136.2 11.5 %copy.43 = bf16[3,512,2048]{2,0,1:T(4,128)(2,1)} copy(bf16[3,512,2048]{2,1,0:T(8,128)(2,1)} %bitcast.91) | data formatting | bytes 12582912 | tf_op jit(solution)/shard_map/all_to_all | solution.py:45
  147.7 24.7 %gather_fusion = bf16[640,3,2048]{2,1,0:T(4,128)(2,1)} fusion(bf16[3,512,2048]{2,0,1:T(4,128)(2,1)} %copy.43, s32[1024]{0:T(1024)S(1)} %pad_clamp_fusion), kind=kCustom, calls=%fused_computation | custom fusion | bytes 15731200 | tf_op jit(solution)/shard_map/jit(_take)/gather | solution.py:46
  172.5 16.3 %copy_select_fusion = bf16[3,16,40,2048]{3,2,0,1:T(8,128)(2,1)} fusion(bf16[3,16,40,2048]{3,0,2,1:T(4,128)(2,1)} %bitcast.88, pred[16,40]{1,0:T(8,128)(4,1)S(1)} %compare_bitcast_fusion), kind=kLoop, calls=%fused_computation.4 | loop fusion | flops 3932160 | bytes 15729280 | tf_op jit(solution)/shard_map/jit(_take)/select_n | solution.py:46
  188.7 6.2 all-to-all-start.1
  198.7 137.9 %all-to-all-done.1 = bf16[3,16,40,2048]{3,2,0,1:T(8,128)(2,1)} async-done(((bf16[3,16,40,2048]{3,2,0,1:T(8,128)(2,1)}), bf16[3,16,40,2048]{3,2,0,1:T(8,128)(2,1)}, u32[]{:S(2)}, u32[]{:S(2)}) %all-to-all-start.1) | async-done | bytes 7864352 | tf_op jit(solution)/shard_map/all_to_all | solution.py:49
  336.6 4.2 copy.45
  340.8 25.5 %copy.46 = bf16[640,3,2048]{2,1,0:T(4,128)(2,1)} copy(bf16[640,3,2048]{2,0,1:T(8,128)(2,1)S(1)} %bitcast.89) | data formatting | bytes 15728640 | tf_op jit(solution)/shard_map/reshape | solution.py:30
  366.3 7.6 broadcast_in_dim.178
  373.9 85.0 %scatter_fusion = bf16[3,512,2048]{2,0,1:T(4,128)(2,1)} fusion(bf16[3,512,2048]{2,0,1:T(4,128)(2,1)} %broadcast_in_dim.178, s32[640]{0:T(1024)S(1)} %fusion.213, bf16[640,3,2048]{2,1,0:T(4,128)(2,1)} %copy.46), kind=kCustom, calls=%fused_computation.1 | custom fusion | bytes 23595520 | tf_op jit(solution)/shard_map/scatter | solution.py:33
  459.0 20.8 %fusion.232 = (bf16[1,512,2048]{2,0,1:T(2,128)(2,1)}, bf16[1,512,2048]{2,0,1:T(2,128)(2,1)}, bf16[1,512,2048]{2,0,1:T(2,128)(2,1)}) fusion(bf16[3,512,2048]{2,0,1:T(4,128)(2,1)} %scatter_fusion), kind=kLoop, calls=%fused_computation.301 | loop fusion | bytes 12582912 | tf_op jit(solution)/shard_map/slice | solution.py:51
  479.8 9.0 %copy.47 = bf16[1,512,2048]{1,2,0:T(8,128)(2,1)S(1)} copy(bf16[1,512,2048]{2,0,1:T(2,128)(2,1)} %get-tuple-element.130) | data formatting | bytes 4194304 | tf_op jit(solution)/shard_map/slice | solution.py:51
  488.8 10.5 %copy.48 = bf16[1,512,2048]{1,2,0:T(8,128)(2,1)} copy(bf16[1,512,2048]{2,0,1:T(2,128)(2,1)} %get-tuple-element.131) | data formatting | bytes 4194304 | tf_op jit(solution)/shard_map/slice | solution.py:51
  499.3 3.3 fusion.1
  504.5 63.3 %all-reduce = f32[16]{0:T(128)S(1)} all-reduce(f32[16]{0:T(128)S(1)} %dynamic-update-slice), channel_id=1, replica_groups=mesh['seq'=16,'head'=2] {'seq'}, use_global_device_ids=true, to_apply=%add | all-reduce | flops 16 | bytes 128
  567.8 3.6 copy.59
  571.5 6.9 copy_bitcast_fusion
  578.4 80.6 %all-gather.3.cloned.1.call-done = f32[256,128,128]{2,1,0:T(8,128)} async-done(((f32[16,128,128]{2,1,0:T(8,128)}), f32[256,128,128]{2,1,0:T(8,128)}) %all-gather.3.cloned.1.call-update) | async-done | bytes 16777232 | tf_op jit(solution)/shard_map/all_gather | solution.py:12
  658.9 54.5 %while.14 = (s32[]{:T(128)}, f32[16,128,128]{2,1,0:T(8,128)S(1)}, s32[]{:T(128)}, f32[16,16,128,128]{3,2,1,0:T(8,128)}, f32[16]{0:T(128)S(1)}, /*index=5*/s32[]{:T(128)}, f32[1]{0:T(128)}, s32[]{:T(128)}) while((s32[]{:T(128)}, f32[16,128,128]{2,1,0:T(8,128)S(1)}, s32[]{:T(128)}, f32[16,16,128,128]{3,2,1,0:T(8,128)}, ...), condition=%wide.region_6.7_spmd.clone, body=%wide.region_5.6_spmd.clone.sunk | while | flops 1048581 | bytes 3145873 | solution.py:24
  660.2 2.1 fusion.300
  663.6 2.1 fusion.300
  667.0 2.1 fusion.300
  670.4 2.1 fusion.300
  673.8 2.1 fusion.300
  677.2 2.1 fusion.300
  680.6 2.1 fusion.300
  684.0 2.1 fusion.300
  687.4 2.1 fusion.300
  690.8 2.1 fusion.300
  694.1 2.1 fusion.300
  697.5 2.1 fusion.300
  700.9 2.1 fusion.300
  704.3 2.1 fusion.300
  707.7 2.1 fusion.300
  711.1 2.1 fusion.300
  718.6 1.0 convolution_select_fusion.24
  721.7 1.0 convolution_select_fusion.27
  724.8 1.0 convolution_select_fusion.30
  728.9 1.0 convolution_select_fusion.18
  729.9 1.7 multiply_reduce_fusion.3
  731.6 2.4 multiply_reduce_fusion.4
  734.1 2.3 multiply_reduce_fusion.5
  736.3 2.3 multiply_reduce_fusion.6
  738.6 2.3 multiply_reduce_fusion.7
  740.9 2.3 multiply_reduce_fusion.8
  743.2 2.3 multiply_reduce_fusion.9
  745.5 2.3 multiply_reduce_fusion.10
  747.8 2.3 multiply_reduce_fusion.11
  750.1 2.3 multiply_reduce_fusion.12
  752.4 2.3 multiply_reduce_fusion.13
  754.7 2.3 multiply_reduce_fusion.14
  757.0 2.3 multiply_reduce_fusion.15
  759.3 2.3 multiply_reduce_fusion
  761.6 2.2 multiply_reduce_fusion.2
  763.8 2.2 multiply_reduce_fusion.1
  766.1 1.1 fusion.69
  767.3 1.1 fusion.70
  769.4 1.1 fusion.72
  770.5 1.1 fusion.73
  772.7 2.4 copy.50
  (137 shorter events, 28.7 us)
Async XLA Ops:
  19.6 7.1 copy-start.25
  19.6 100.9 %all-to-all-start = ((bf16[3,256,4096]{1,0,2:T(4,128)(2,1)}), bf16[3,256,4096]{1,0,2:T(4,128)(2,1)}, u32[]{:S(2)}, u32[]{:S(2)}) async-start(bf16[3,256,4096]{1,0,2:T(4,128)(2,1)} %copy.40), calls=%async_computation | async-start | bytes 16777216 | tf_op jit(solution)/shard_map/all_to_all | solution.py:45
  188.7 6.3 copy-start.28
  188.7 7.8 %copy-start.26 = (s32[1,16,40]{2,1,0:T(8,128)S(1)}, s32[1,16,40]{2,1,0:T(8,128)}, u32[]{:S(2)}) copy-start(s32[1,16,40]{2,1,0:T(8,128)} %param.9) | copy-start | bytes 7684
  188.7 147.8 %all-to-all-start.1 = ((bf16[3,16,40,2048]{3,2,0,1:T(8,128)(2,1)}), bf16[3,16,40,2048]{3,2,0,1:T(8,128)(2,1)}, u32[]{:S(2)}, u32[]{:S(2)}) async-start(bf16[3,16,40,2048]{3,2,0,1:T(8,128)(2,1)} %copy_select_fusion), calls=%async_computation.1 | async-start | bytes 15728640 | tf_op jit(solution)/shard_map/all_to_all | solution.py:49
  195.0 464.0 %all-gather.3.cloned.1.call-start = ((), (), s32[]{:S(2)}) async-start(), calls=%async_computation.2 | async-start | bytes 17825792 | tf_op jit(solution)/shard_map/all_gather | solution.py:12
  499.3 3.3 copy-start.29
  499.3 68.5 %copy-start.27 = (f32[2048]{0:T(1024)S(1)}, f32[2048]{0:T(1024)}, u32[]{:S(2)}) copy-start(f32[2048]{0:T(1024)} %param.11) | copy-start | bytes 24580
  567.8 3.7 copy-start
  729.9 4.1 copy-start.24
  731.6 4.7 copy-start.23
  734.0 4.6 copy-start.22
  736.3 4.6 copy-start.21
  738.6 4.6 copy-start.20
  740.9 4.6 copy-start.19
  743.2 4.6 copy-start.18
  745.5 4.6 copy-start.17
  747.8 4.6 copy-start.16
  750.1 4.6 copy-start.15
  752.4 4.6 copy-start.14
  754.7 4.6 copy-start.13
  757.0 4.6 copy-start.12
  759.3 4.5 copy-start.11
  766.0 5.5 copy-start.10
  766.1 5.6 copy-start.7
  766.1 5.7 copy-start.6
  766.1 5.8 copy-start.4
  766.1 5.9 copy-start.3
  766.1 6.0 copy-start.2
  767.3 5.0 copy-start.1
  769.4 3.0 copy-start.9
  770.5 2.0 copy-start.8
  771.6 1.0 copy-start.5
Sparse Core Ops, SparseCore 0:
  502.7 156.1 all-gather.2
where the time goes:
time: 794 us; the launch traced here: 782 us
  waiting for transfers between devices  312 us (39%)
  local copies, waits for them, and re-layouts  253 us (32%)
  blocking collectives  63.3 us (8%)
  other arithmetic  59.2 us (7%)
  matrix products  55.6 us (7%)
  between operations  15.6 us (2%)
  starting transfers between devices  13.3 us (2%)
  loops' own time  10.4 us (1%)
    all_to_all x1, waiting for transfers between devices, on_device(): lax.all_to_all(outgoing, 'seq', split_axis=1, concat_axis=1, tiled=True)  138 us
    all_to_all x1, waiting for transfers between devices, on_device(): lax.all_to_all(qkv, 'head', split_axis=2, concat_axis=1, tiled=True)  93.7 us
    scatter x1, local copies, waits for them, and re-layouts, place_rows(): return blank_rows.at[:, land_index].set(flat_rows, mode='drop')  85 us
    all_gather x1, waiting for transfers between devices, prefix(): everything = jax.tree.map(lambda part: lax.all_gather(part, axis), shard)  80.6 us
    unnamed x1, blocking collectives  63.3 us
    slice x3, local copies, waits for them, and re-layouts, on_device(): query, keys, values = (packed[0], packed[1], packed[2])  40.3 us
    dot_general x16, matrix products, on_device(): jnp.dot(weights, value_head, preferred_element_type=jnp.float32)  35.8 us
    select_n x16, other arithmetic, lap(): return jax.tree.map(lambda a, b: jnp.where(reached, a, b), new, before)  34.2 us
  transfers between devices with their start and end apart: 3, of which 3 were waited for; matrix products, arithmetic and copies ran while one was open for 2% of the time, Pallas kernels for 0%

commit v1 on v0

--- a/solution.py
+++ b/solution.py
@@ -5,6 +5,28 @@
 
 HEAD_DIM = 128
 norm_eps = 1e-06
+
+
+def in_blocks(array, dim, size):
+    before, after = (array.shape[:dim], array.shape[dim + 1 :])
+    return jnp.moveaxis(array.reshape(*before, size, -1, *after), dim, 0)
+
+
+def laid_out(blocks, dim):
+    dims = list(blocks.shape[1:])
+    dims[dim] *= blocks.shape[0]
+    return jnp.moveaxis(blocks, 0, dim).reshape(dims)
+
+
+def rotated_exchange(x, axis, split_dim, concat_dim):
+    peers, index = (lax.axis_size(axis), lax.axis_index(axis))
+    parts = in_blocks(x, split_dim, peers)
+    outs = [parts[index]]
+    for step in range(1, peers):
+        sent = parts[(index + step) % peers]
+        outs.append(lax.ppermute(sent, axis, [(i, (i + step) % peers) for i in range(peers)]))
+    parts = jnp.stack(outs)[(index - jnp.arange(peers)) % peers]
+    return laid_out(parts, concat_dim)
 
 
 def prefix(shard, axis, combine, identity):
@@ -46,7 +68,7 @@
     outgoing = jnp.take(grouped, pick_rows, axis=1).reshape(
         3, seq_count, slot_count, grouped.shape[2]
     )
-    arrived = lax.all_to_all(outgoing, "seq", split_axis=1, concat_axis=1, tiled=True)
+    arrived = rotated_exchange(outgoing, "seq", 1, 1)
     packed = place_rows(arrived, land_rows, grouped.shape[1])
     query, keys, values = (packed[0], packed[1], packed[2])
     tok_rows = keys.shape[0]

time: 794 us -> 819 us (1.031)
  starting transfers between devices: 13.3 us -> 91.6 us
  waiting for transfers between devices: 312 us -> 250 us
  local copies, waits for them, and re-layouts: 253 us -> 297 us
  blocking collectives: 63.3 us -> 34.7 us
  other arithmetic: 59.2 us -> 50.6 us
    all_to_all x1 -> x0, waiting for transfers between devices: 138 us -> none  [on_device(): lax.all_to_all(outgoing, 'seq', split_axis=1, concat_axis=1, tiled=True)]
    ppermute x0 -> x15, starting transfers between devices: none -> 84.5 us  [rotated_exchange(): lax.ppermute(sent, axis, [(i, (i + step) % peers) for i in range(peers)])]
    ppermute x0 -> x15, waiting for transfers between devices: none -> 79.1 us  [rotated_exchange(): lax.ppermute(sent, axis, [(i, (i + step) % peers) for i in range(peers)])]
    another operation x0 -> x18, local copies, waits for them, and re-layouts: none -> 38.1 us  [the longest x1 25.3 us: place_rows(): flat_rows = incoming.reshape(planes, -1, row_width)]
    unnamed x1, blocking collectives: 63.3 us -> 34.7 us
    reshape x1 -> x0, local copies, waits for them, and re-layouts: 25.5 us -> none  [place_rows(): flat_rows = incoming.reshape(planes, -1, row_width)]
    gather x0 -> x1, local copies, waits for them, and re-layouts: none -> 18.2 us  [rotated_exchange(): parts = jnp.stack(outs)[(index - jnp.arange(peers)) % peers]]
    unnamed x66 -> x81, local copies, waits for them, and re-layouts: 25 us -> 38 us
  transfers between devices with their start and end apart: 3 -> 17, of which waited for: 3 -> 7; matrix products, arithmetic and copies ran while one was open for 2% -> 4% of each run, Pallas kernels for 0% -> 0%
where the time goes in v1:
time: 819 us; the launch traced here: 807 us
  local copies, waits for them, and re-layouts  297 us (36%)
  waiting for transfers between devices  250 us (31%)
  starting transfers between devices  91.6 us (11%)
  matrix products  55.2 us (7%)
  other arithmetic  50.6 us (6%)
  blocking collectives  34.7 us (4%)
  between operations  16.1 us (2%)
  loops' own time  11.7 us (1%)
    all_to_all x1, waiting for transfers between devices, on_device(): lax.all_to_all(qkv, 'head', split_axis=2, concat_axis=1, tiled=True)  89.6 us
    scatter x1, local copies, waits for them, and re-layouts, place_rows(): return blank_rows.at[:, land_index].set(flat_rows, mode='drop')  85.1 us
    ppermute x15, starting transfers between devices, rotated_exchange(): lax.ppermute(sent, axis, [(i, (i + step) % peers) for i in range(peers)])  84.5 us
    all_gather x1, waiting for transfers between devices, prefix(): everything = jax.tree.map(lambda part: lax.all_gather(part, axis), shard)  81.7 us
    ppermute x15, waiting for transfers between devices, rotated_exchange(): lax.ppermute(sent, axis, [(i, (i + step) % peers) for i in range(peers)])  79.1 us
    slice x3, local copies, waits for them, and re-layouts, on_device(): query, keys, values = (packed[0], packed[1], packed[2])  40.2 us
    unnamed x81, local copies, waits for them, and re-layouts  38 us
    dot_general x16, matrix products, on_device(): jnp.dot(weights, value_head, preferred_element_type=jnp.float32)  35.7 us
  transfers between devices with their start and end apart: 17, of which 7 were waited for; matrix products, arithmetic and copies ran while one was open for 4% of the time, Pallas kernels for 0%

profile of v1, /device:TPU:0, one launch (start us, length us, event | category | flops | bytes accessed | tf_op | source)
XLA Modules:
  0.0 807.0 jit_solution(13320864263169126828)
XLA Ops:
  6.5 13.1 %copy.80 = bf16[3,256,4096]{1,0,2:T(4,128)(2,1)} copy(bf16[3,256,4096]{2,1,0:T(8,128)(2,1)} %param.7) | data formatting | bytes 12582912 | tf_op args[0]
  19.6 7.1 all-to-all-start
  30.9 89.6 %all-to-all-done = bf16[3,256,4096]{1,0,2:T(4,128)(2,1)} async-done(((bf16[3,256,4096]{1,0,2:T(4,128)(2,1)}), bf16[3,256,4096]{1,0,2:T(4,128)(2,1)}, u32[]{:S(2)}, u32[]{:S(2)}) %all-to-all-start) | async-done | bytes 6291488 | tf_op jit(solution)/shard_map/all_to_all | solution.py:67
  120.6 7.0 copy.81
  127.5 8.7 %copy.82 = bf16[3,2,256,2048]{3,2,1,0:T(8,128)(2,1)} copy(bf16[3,2,256,2048]{2,3,1,0:T(8,128)(2,1)} %bitcast.174) | data formatting | bytes 12582912 | tf_op jit(solution)/shard_map/all_to_all | solution.py:67
  136.2 11.5 %copy.83 = bf16[3,512,2048]{2,0,1:T(4,128)(2,1)} copy(bf16[3,512,2048]{2,1,0:T(8,128)(2,1)} %bitcast.175) | data formatting | bytes 12582912 | tf_op jit(solution)/shard_map/all_to_all | solution.py:67
  147.7 24.3 %gather_fusion = bf16[640,3,2048]{2,1,0:T(4,128)(2,1)} fusion(bf16[3,512,2048]{2,0,1:T(4,128)(2,1)} %copy.83, s32[1024]{0:T(1024)S(1)} %pad_clamp_fusion.1), kind=kCustom, calls=%fused_computation | custom fusion | bytes 15731200 | tf_op jit(solution)/shard_map/jit(_take)/gather | solution.py:68
  172.0 7.5 broadcast_select_fusion
  179.5 6.5 constant_dynamic-slice_fusion
  189.7 2.5 collective-permute-start.2
  201.4 3.6 collective-permute-done.1
  205.0 5.7 collective-permute-start.6
  211.6 2.6 collective-permute-start.7
  215.0 3.4 collective-permute-start.8
  219.3 67.6 %collective-permute-done.4 = bf16[3,1,40,2048]{3,2,0,1:T(8,128)(2,1)S(1)} collective-permute-done((bf16[3,1,40,2048]{3,2,0,1:T(8,128)(2,1)S(1)}, bf16[3,1,40,2048]{3,2,0,1:T(8,128)(2,1)S(1)}, u32[]{:S(2)}, u32[]{:S(2)}) %collective-permute-start.4) | collective-permute-done | bytes 491552 | tf_op jit(solution)/shard_map/ppermute | solution.py:27
  287.7 13.5 %collective-permute-start.10 = (bf16[3,1,40,2048]{3,2,0,1:T(8,128)(2,1)S(1)}, bf16[3,1,40,2048]{3,2,0,1:T(8,128)(2,1)S(1)}, u32[]{:S(2)}, u32[]{:S(2)}) collective-permute-start(bf16[3,1,40,2048]{3,2,0,1:T(8,128)(2,1)S(1)} %bitcast.215), channel_id=1, source_target_pairs={{0,22},{2,24},{4,26},{6,28},{8,30},{10,0},{12,2},{14,4},{16,6},{18... | collective-permute-start | bytes 1474568 | tf_op jit(solution)/shard_map/ppermute | solution.py:27
  302.0 21.5 %collective-permute-start.11 = (bf16[3,1,40,2048]{3,2,0,1:T(8,128)(2,1)S(1)}, bf16[3,1,40,2048]{3,2,0,1:T(8,128)(2,1)S(1)}, u32[]{:S(2)}, u32[]{:S(2)}) collective-permute-start(bf16[3,1,40,2048]{3,2,0,1:T(8,128)(2,1)S(1)} %bitcast.214), channel_id=1, source_target_pairs={{0,24},{2,26},{4,28},{6,30},{8,0},{10,2},{12,4},{14,6},{16,8},{18,... | collective-permute-start | bytes 1474568 | tf_op jit(solution)/shard_map/ppermute | solution.py:27
  324.4 3.8 collective-permute-start.12
  328.9 15.6 %collective-permute-start.13 = (bf16[3,1,40,2048]{3,2,0,1:T(8,128)(2,1)S(1)}, bf16[3,1,40,2048]{3,2,0,1:T(8,128)(2,1)S(1)}, u32[]{:S(2)}, u32[]{:S(2)}) collective-permute-start(bf16[3,1,40,2048]{3,2,0,1:T(8,128)(2,1)S(1)} %bitcast.212), channel_id=1, source_target_pairs={{0,28},{2,30},{4,0},{6,2},{8,4},{10,6},{12,8},{14,10},{16,12},{18,... | collective-permute-start | bytes 1474568 | tf_op jit(solution)/shard_map/ppermute | solution.py:27
  345.3 12.5 %collective-permute-start.14 = (bf16[3,1,40,2048]{3,2,0,1:T(8,128)(2,1)S(1)}, bf16[3,1,40,2048]{3,2,0,1:T(8,128)(2,1)S(1)}, u32[]{:S(2)}, u32[]{:S(2)}) collective-permute-start(bf16[3,1,40,2048]{3,2,0,1:T(8,128)(2,1)S(1)} %bitcast.211), channel_id=1, source_target_pairs={{0,30},{2,0},{4,2},{6,4},{8,6},{10,8},{12,10},{14,12},{16,14},{18,... | collective-permute-start | bytes 1474568 | tf_op jit(solution)/shard_map/ppermute | solution.py:27
  363.8 4.2 collective-permute-done.14
  368.8 18.2 %gather_fusion.1 = bf16[16,3,40,2048]{3,2,1,0:T(8,128)(2,1)} fusion(bf16[16,3,40,2048]{3,2,1,0:T(8,128)(2,1)} %bitcast.39, s32[1024]{0:T(1024)S(1)} %pad_clamp_fusion), kind=kCustom, calls=%fused_computation.1 | custom fusion | bytes 15728704 | tf_op jit(solution)/shard_map/gather | solution.py:28
  387.1 4.2 copy.100
  391.3 25.3 %copy.101 = bf16[640,3,2048]{2,1,0:T(4,128)(2,1)} copy(bf16[640,3,2048]{2,0,1:T(8,128)(2,1)S(1)} %bitcast.173) | data formatting | bytes 15728640 | tf_op jit(solution)/shard_map/reshape;reshape | solution.py:52
  416.6 7.6 broadcast_in_dim.179
  424.2 85.1 %scatter_fusion = bf16[3,512,2048]{2,0,1:T(4,128)(2,1)} fusion(bf16[3,512,2048]{2,0,1:T(4,128)(2,1)} %broadcast_in_dim.179, s32[640]{0:T(1024)S(1)} %fusion.213, bf16[640,3,2048]{2,1,0:T(4,128)(2,1)} %copy.101), kind=kCustom, calls=%fused_computation.2 | custom fusion | bytes 23595520 | tf_op jit(solution)/shard_map/scatter | solution.py:55
  509.3 20.8 %fusion.234 = (bf16[1,512,2048]{2,0,1:T(2,128)(2,1)}, bf16[1,512,2048]{2,0,1:T(2,128)(2,1)}, bf16[1,512,2048]{2,0,1:T(2,128)(2,1)}) fusion(bf16[3,512,2048]{2,0,1:T(4,128)(2,1)} %scatter_fusion), kind=kLoop, calls=%fused_computation.356 | loop fusion | bytes 12582912 | tf_op jit(solution)/shard_map/slice | solution.py:73
  530.1 9.0 %copy.102 = bf16[1,512,2048]{1,2,0:T(8,128)(2,1)S(1)} copy(bf16[1,512,2048]{2,0,1:T(2,128)(2,1)} %get-tuple-element.146) | data formatting | bytes 4194304 | tf_op jit(solution)/shard_map/slice | solution.py:73
  539.0 10.5 %copy.103 = bf16[1,512,2048]{1,2,0:T(8,128)(2,1)} copy(bf16[1,512,2048]{2,0,1:T(2,128)(2,1)} %get-tuple-element.147) | data formatting | bytes 4194304 | tf_op jit(solution)/shard_map/slice | solution.py:73
  549.5 3.3 fusion.1
  555.0 34.7 %all-reduce = f32[16]{0:T(128)S(1)} all-reduce(f32[16]{0:T(128)S(1)} %dynamic-update-slice), channel_id=1, replica_groups=mesh['seq'=16,'head'=2] {'seq'}, use_global_device_ids=true, to_apply=%add | all-reduce | flops 16 | bytes 128
  589.8 3.6 copy.129
  593.4 6.9 copy_bitcast_fusion
  600.3 81.7 %all-gather.3.cloned.1.call-done = f32[256,128,128]{2,1,0:T(8,128)} async-done(((f32[16,128,128]{2,1,0:T(8,128)}), f32[256,128,128]{2,1,0:T(8,128)}) %all-gather.3.cloned.1.call-update) | async-done | bytes 16777232 | tf_op jit(solution)/shard_map/all_gather | solution.py:34
  682.0 56.6 %while.14 = (s32[]{:T(128)}, f32[16,128,128]{2,1,0:T(8,128)S(1)}, s32[]{:T(128)}, f32[16,16,128,128]{3,2,1,0:T(8,128)}, f32[16]{0:T(128)S(1)}, /*index=5*/s32[]{:T(128)}, f32[1]{0:T(128)}, s32[]{:T(128)}) while((s32[]{:T(128)}, f32[16,128,128]{2,1,0:T(8,128)S(1)}, s32[]{:T(128)}, f32[16,16,128,128]{3,2,1,0:T(8,128)}, ...), condition=%wide.region_6.7_spmd.clone, body=%wide.region_5.6_spmd.clone.sunk | while | flops 1048581 | bytes 3145873 | solution.py:46
  683.3 2.1 fusion.302
  686.8 2.1 fusion.302
  690.4 2.1 fusion.302
  693.9 2.1 fusion.302
  697.4 2.1 fusion.302
  700.9 2.1 fusion.302
  704.5 2.1 fusion.302
  708.0 2.1 fusion.302
  711.5 2.1 fusion.302
  715.0 2.1 fusion.302
  722.1 2.1 fusion.302
  729.1 2.1 fusion.302
  736.2 2.1 fusion.302
  756.5 2.4 multiply_reduce_fusion.4
  758.9 2.3 multiply_reduce_fusion.5
  761.2 2.3 multiply_reduce_fusion.6
  763.5 2.3 multiply_reduce_fusion.7
  765.7 2.3 multiply_reduce_fusion.8
  768.0 2.3 multiply_reduce_fusion.9
  770.3 2.3 multiply_reduce_fusion.10
  772.6 2.3 multiply_reduce_fusion.11
  774.9 2.3 multiply_reduce_fusion.12
  777.2 2.3 multiply_reduce_fusion.13
  779.4 2.3 multiply_reduce_fusion.14
  781.7 2.3 multiply_reduce_fusion.15
  784.0 2.3 multiply_reduce_fusion
  786.3 2.2 multiply_reduce_fusion.2
  788.5 2.2 multiply_reduce_fusion.1
  797.4 2.4 copy.105
  (200 shorter events, 72.4 us)
Async XLA Ops:
  19.6 7.3 copy-start.28
  19.6 8.9 %copy-start.26 = (s32[1,16,40]{2,1,0:T(8,128)S(1)}, s32[1,16,40]{2,1,0:T(8,128)}, u32[]{:S(2)}) copy-start(s32[1,16,40]{2,1,0:T(8,128)} %param.9) | copy-start | bytes 7684
  19.6 9.0 %copy-start.25 = (s32[1,16,40]{2,1,0:T(8,128)S(1)}, s32[1,16,40]{2,1,0:T(8,128)}, u32[]{:S(2)}) copy-start(s32[1,16,40]{2,1,0:T(8,128)} %param.8) | copy-start | bytes 7684
  19.6 101.0 %all-to-all-start = ((bf16[3,256,4096]{1,0,2:T(4,128)(2,1)}), bf16[3,256,4096]{1,0,2:T(4,128)(2,1)}, u32[]{:S(2)}, u32[]{:S(2)}) async-start(bf16[3,256,4096]{1,0,2:T(4,128)(2,1)} %copy.80), calls=%async_computation | async-start | bytes 16777216 | tf_op jit(solution)/shard_map/all_to_all | solution.py:67
  26.7 655.3 %all-gather.3.cloned.1.call-start = ((), (), s32[]{:S(2)}) async-start(), calls=%async_computation.1 | async-start | bytes 17825792 | tf_op jit(solution)/shard_map/all_gather | solution.py:34
  186.4 14.2 %collective-permute-start = (bf16[3,1,40,2048]{3,2,0,1:T(8,128)(2,1)S(1)}, bf16[3,1,40,2048]{3,2,0,1:T(8,128)(2,1)S(1)}, u32[]{:S(2)}, u32[]{:S(2)}) collective-permute-start(bf16[3,1,40,2048]{3,2,0,1:T(8,128)(2,1)S(1)} %bitcast.224), channel_id=1, source_target_pairs={{0,2},{2,4},{4,6},{6,8},{8,10},{10,12},{12,14},{14,16},{16,18},{18... | collective-permute-start | bytes 1474568 | tf_op jit(solution)/shard_map/ppermute | solution.py:27
  188.0 17.0 %collective-permute-start.1 = (bf16[3,1,40,2048]{3,2,0,1:T(8,128)(2,1)S(1)}, bf16[3,1,40,2048]{3,2,0,1:T(8,128)(2,1)S(1)}, u32[]{:S(2)}, u32[]{:S(2)}) collective-permute-start(bf16[3,1,40,2048]{3,2,0,1:T(8,128)(2,1)S(1)} %bitcast.225), channel_id=1, source_target_pairs={{0,4},{2,6},{4,8},{6,10},{8,12},{10,14},{12,16},{14,18},{16,20},{1... | collective-permute-start | bytes 1474568 | tf_op jit(solution)/shard_map/ppermute | solution.py:27
  189.7 21.9 %collective-permute-start.2 = (bf16[3,1,40,2048]{3,2,0,1:T(8,128)(2,1)S(1)}, bf16[3,1,40,2048]{3,2,0,1:T(8,128)(2,1)S(1)}, u32[]{:S(2)}, u32[]{:S(2)}) collective-permute-start(bf16[3,1,40,2048]{3,2,0,1:T(8,128)(2,1)S(1)} %bitcast.222), channel_id=1, source_target_pairs={{0,6},{2,8},{4,10},{6,12},{8,14},{10,16},{12,18},{14,20},{16,22},{... | collective-permute-start | bytes 1474568 | tf_op jit(solution)/shard_map/ppermute | solution.py:27
  192.1 22.9 %collective-permute-start.3 = (bf16[3,1,40,2048]{3,2,0,1:T(8,128)(2,1)S(1)}, bf16[3,1,40,2048]{3,2,0,1:T(8,128)(2,1)S(1)}, u32[]{:S(2)}, u32[]{:S(2)}) collective-permute-start(bf16[3,1,40,2048]{3,2,0,1:T(8,128)(2,1)S(1)} %bitcast.220), channel_id=1, source_target_pairs={{0,8},{2,10},{4,12},{6,14},{8,16},{10,18},{12,20},{14,22},{16,24},... | collective-permute-start | bytes 1474568 | tf_op jit(solution)/shard_map/ppermute | solution.py:27
  193.7 93.2 %collective-permute-start.4 = (bf16[3,1,40,2048]{3,2,0,1:T(8,128)(2,1)S(1)}, bf16[3,1,40,2048]{3,2,0,1:T(8,128)(2,1)S(1)}, u32[]{:S(2)}, u32[]{:S(2)}) collective-permute-start(bf16[3,1,40,2048]{3,2,0,1:T(8,128)(2,1)S(1)} %bitcast.218), channel_id=1, source_target_pairs={{0,10},{2,12},{4,14},{6,16},{8,18},{10,20},{12,22},{14,24},{16,26}... | collective-permute-start | bytes 1474568 | tf_op jit(solution)/shard_map/ppermute | solution.py:27
  200.6 87.1 %collective-permute-start.5 = (bf16[3,1,40,2048]{3,2,0,1:T(8,128)(2,1)S(1)}, bf16[3,1,40,2048]{3,2,0,1:T(8,128)(2,1)S(1)}, u32[]{:S(2)}, u32[]{:S(2)}) collective-permute-start(bf16[3,1,40,2048]{3,2,0,1:T(8,128)(2,1)S(1)} %bitcast.223), channel_id=1, source_target_pairs={{0,12},{2,14},{4,16},{6,18},{8,20},{10,22},{12,24},{14,26},{16,28}... | collective-permute-start | bytes 1474568 | tf_op jit(solution)/shard_map/ppermute | solution.py:27
  205.0 97.0 %collective-permute-start.6 = (bf16[3,1,40,2048]{3,2,0,1:T(8,128)(2,1)S(1)}, bf16[3,1,40,2048]{3,2,0,1:T(8,128)(2,1)S(1)}, u32[]{:S(2)}, u32[]{:S(2)}) collective-permute-start(bf16[3,1,40,2048]{3,2,0,1:T(8,128)(2,1)S(1)} %bitcast.221), channel_id=1, source_target_pairs={{0,14},{2,16},{4,18},{6,20},{8,22},{10,24},{12,26},{14,28},{16,30}... | collective-permute-start | bytes 1474568 | tf_op jit(solution)/shard_map/ppermute | solution.py:27
  211.6 112.8 %collective-permute-start.7 = (bf16[3,1,40,2048]{3,2,0,1:T(8,128)(2,1)S(1)}, bf16[3,1,40,2048]{3,2,0,1:T(8,128)(2,1)S(1)}, u32[]{:S(2)}, u32[]{:S(2)}) collective-permute-start(bf16[3,1,40,2048]{3,2,0,1:T(8,128)(2,1)S(1)} %bitcast.219), channel_id=1, source_target_pairs={{0,16},{2,18},{4,20},{6,22},{8,24},{10,26},{12,28},{14,30},{16,0},... | collective-permute-start | bytes 1474568 | tf_op jit(solution)/shard_map/ppermute | solution.py:27
  215.0 113.9 %collective-permute-start.8 = (bf16[3,1,40,2048]{3,2,0,1:T(8,128)(2,1)S(1)}, bf16[3,1,40,2048]{3,2,0,1:T(8,128)(2,1)S(1)}, u32[]{:S(2)}, u32[]{:S(2)}) collective-permute-start(bf16[3,1,40,2048]{3,2,0,1:T(8,128)(2,1)S(1)} %bitcast.217), channel_id=1, source_target_pairs={{0,18},{2,20},{4,22},{6,24},{8,26},{10,28},{12,30},{14,0},{16,2},{... | collective-permute-start | bytes 1474568 | tf_op jit(solution)/shard_map/ppermute | solution.py:27
  286.9 58.5 %collective-permute-start.9 = (bf16[3,1,40,2048]{3,2,0,1:T(8,128)(2,1)S(1)}, bf16[3,1,40,2048]{3,2,0,1:T(8,128)(2,1)S(1)}, u32[]{:S(2)}, u32[]{:S(2)}) collective-permute-start(bf16[3,1,40,2048]{3,2,0,1:T(8,128)(2,1)S(1)} %bitcast.216), channel_id=1, source_target_pairs={{0,20},{2,22},{4,24},{6,26},{8,28},{10,30},{12,0},{14,2},{16,4},{1... | collective-permute-start | bytes 1474568 | tf_op jit(solution)/shard_map/ppermute | solution.py:27
  287.7 71.0 %collective-permute-start.10 = (bf16[3,1,40,2048]{3,2,0,1:T(8,128)(2,1)S(1)}, bf16[3,1,40,2048]{3,2,0,1:T(8,128)(2,1)S(1)}, u32[]{:S(2)}, u32[]{:S(2)}) collective-permute-start(bf16[3,1,40,2048]{3,2,0,1:T(8,128)(2,1)S(1)} %bitcast.215), channel_id=1, source_target_pairs={{0,22},{2,24},{4,26},{6,28},{8,30},{10,0},{12,2},{14,4},{16,6},{18... | collective-permute-start | bytes 1474568 | tf_op jit(solution)/shard_map/ppermute | solution.py:27
  302.0 57.5 %collective-permute-start.11 = (bf16[3,1,40,2048]{3,2,0,1:T(8,128)(2,1)S(1)}, bf16[3,1,40,2048]{3,2,0,1:T(8,128)(2,1)S(1)}, u32[]{:S(2)}, u32[]{:S(2)}) collective-permute-start(bf16[3,1,40,2048]{3,2,0,1:T(8,128)(2,1)S(1)} %bitcast.214), channel_id=1, source_target_pairs={{0,24},{2,26},{4,28},{6,30},{8,0},{10,2},{12,4},{14,6},{16,8},{18,... | collective-permute-start | bytes 1474568 | tf_op jit(solution)/shard_map/ppermute | solution.py:27
  324.4 36.0 %collective-permute-start.12 = (bf16[3,1,40,2048]{3,2,0,1:T(8,128)(2,1)S(1)}, bf16[3,1,40,2048]{3,2,0,1:T(8,128)(2,1)S(1)}, u32[]{:S(2)}, u32[]{:S(2)}) collective-permute-start(bf16[3,1,40,2048]{3,2,0,1:T(8,128)(2,1)S(1)} %bitcast.213), channel_id=1, source_target_pairs={{0,26},{2,28},{4,30},{6,0},{8,2},{10,4},{12,6},{14,8},{16,10},{18,... | collective-permute-start | bytes 1474568 | tf_op jit(solution)/shard_map/ppermute | solution.py:27
  328.9 34.0 %collective-permute-start.13 = (bf16[3,1,40,2048]{3,2,0,1:T(8,128)(2,1)S(1)}, bf16[3,1,40,2048]{3,2,0,1:T(8,128)(2,1)S(1)}, u32[]{:S(2)}, u32[]{:S(2)}) collective-permute-start(bf16[3,1,40,2048]{3,2,0,1:T(8,128)(2,1)S(1)} %bitcast.212), channel_id=1, source_target_pairs={{0,28},{2,30},{4,0},{6,2},{8,4},{10,6},{12,8},{14,10},{16,12},{18,... | collective-permute-start | bytes 1474568 | tf_op jit(solution)/shard_map/ppermute | solution.py:27
  345.3 22.7 %collective-permute-start.14 = (bf16[3,1,40,2048]{3,2,0,1:T(8,128)(2,1)S(1)}, bf16[3,1,40,2048]{3,2,0,1:T(8,128)(2,1)S(1)}, u32[]{:S(2)}, u32[]{:S(2)}) collective-permute-start(bf16[3,1,40,2048]{3,2,0,1:T(8,128)(2,1)S(1)} %bitcast.211), channel_id=1, source_target_pairs={{0,30},{2,0},{4,2},{6,4},{8,6},{10,8},{12,10},{14,12},{16,14},{18,... | collective-permute-start | bytes 1474568 | tf_op jit(solution)/shard_map/ppermute | solution.py:27
  549.5 3.4 copy-start.29
  549.5 40.2 %copy-start.27 = (f32[2048]{0:T(1024)S(1)}, f32[2048]{0:T(1024)}, u32[]{:S(2)}) copy-start(f32[2048]{0:T(1024)} %param.11) | copy-start | bytes 24580
  589.8 3.6 copy-start
  754.8 4.1 copy-start.24
  756.5 4.7 copy-start.23
  758.9 4.6 copy-start.22
  761.2 4.6 copy-start.21
  763.5 4.6 copy-start.20
  765.7 4.6 copy-start.19
  768.0 4.6 copy-start.18
  770.3 4.6 copy-start.17
  772.6 4.6 copy-start.16
  774.8 4.6 copy-start.15
  777.1 4.6 copy-start.14
  779.4 4.6 copy-start.13
  781.7 4.6 copy-start.12
  784.0 4.5 copy-start.11
  790.7 5.5 copy-start.10
  790.7 5.6 copy-start.7
  790.7 5.7 copy-start.6
  790.8 5.8 copy-start.4
  790.8 5.9 copy-start.3
  790.8 6.0 copy-start.2
  792.0 5.0 copy-start.1
  794.1 3.0 copy-start.9
  795.2 2.0 copy-start.8
  796.3 1.0 copy-start.5
Sparse Core Ops, SparseCore 0:
  553.0 128.8 all-gather.2
